TPU v7x, 32 devices: a whole 2x2x4 slice. The times are simulated.
32 devices in a mesh: streams: 8 (over z, x), tm: 4 (over y, core).
Axes of the slice: x: 2, y: 2, z: 4, core: 2. Of those that a mesh axis runs over, the one named last changes fastest.
Arguments:
- signal: float32 [2, 2097152], P(None, ('streams', 'tm')), parts along dimension 1, may hold values from -6 to 6
- coarse_taps: float32 [16, 64], replicated, may hold values from -1.5 to 1.5
- fine_taps: float32 [12, 512], replicated, may hold values from -1.8 to 1.8
Outputs:
- channelized: float32 [2, 64, 64, 512], P(None, 'tm', 'streams'), parts along dimension 2
There are 8 independent parts, one for each index of `streams`. A program takes and returns all parts, laid end to end along the dimension named above; an argument that names none is the same for every part. Nothing has to cross between parts.
All inputs are finite; a program needn't handle non-finite values.
Results may differ from a plain program's by a relative error of at most 0.00007.
Values sent between devices are 32-bit elements; how exact they have to be, the bound alone decides.
No kernel may reach another device: no remote copies, remote signals or barrier semaphores. Data moves between devices by JAX's collectives and lax.ppermute only.
A program may use at most 320 MiB of HBM per device.

v0:
```python
import math
import jax
import jax.numpy as jnp
from jax import lax
from jax.sharding import PartitionSpec as P

CHANNELS = 64
FINE = 512
TAPS = 16
FINE_TAPS = 12


def from_behind(array, axis, by):
    length = lax.axis_size(axis)
    pairs = [(i, i + by) for i in range(length) if 0 <= i + by < length]
    return lax.ppermute(array, axis, pairs)


def tables(points):
    counter = jnp.arange(points, dtype=jnp.int32)
    product = counter[:, None] * counter[None, :] % points
    angle = product.astype(jnp.float32) * (2.0 * math.pi / points)
    return (jnp.cos(angle), jnp.sin(angle))


def coarse_branches(extended, coarse_taps, length):
    row_count = length // (2 * CHANNELS)
    summed = jnp.zeros((2, row_count, 2 * CHANNELS), jnp.float32)
    for tap_index in range(TAPS):
        offset = (TAPS - 1 - tap_index) * CHANNELS
        segment = extended[:, offset : offset + length].reshape(2, row_count, 2 * CHANNELS)
        summed = summed + segment * jnp.tile(coarse_taps[tap_index], 2)
    return summed.reshape(2, length // CHANNELS, CHANNELS)


def coarse_spectrum(branches, cosine_rows, sine_rows):
    factor = 1.0 / math.sqrt(CHANNELS)
    highest = lax.Precision.HIGHEST
    real_part = (
        jnp.einsum("kp,tp->kt", cosine_rows, branches[0], precision=highest)
        + jnp.einsum("kp,tp->kt", sine_rows, branches[1], precision=highest)
    ) * factor
    imag_part = (
        jnp.einsum("kp,tp->kt", cosine_rows, branches[1], precision=highest)
        - jnp.einsum("kp,tp->kt", sine_rows, branches[0], precision=highest)
    ) * factor
    return jnp.stack([real_part, imag_part])


def fine_section(coarse, fine_taps):
    group_size = coarse.shape[1]
    fine_frames = coarse.shape[2] // FINE
    shaped = coarse.reshape(2, group_size, fine_frames, FINE)
    padded = jnp.pad(shaped, ((0, 0), (0, 0), (FINE_TAPS - 1, 0), (0, 0)))
    summed = jnp.zeros((2, group_size, fine_frames, FINE), jnp.float32)
    for tap_index in range(FINE_TAPS):
        offset = FINE_TAPS - 1 - tap_index
        summed = summed + fine_taps[tap_index] * padded[:, :, offset : offset + fine_frames, :]
    cosine_table, sine_table = tables(FINE)
    factor = 1.0 / math.sqrt(FINE)
    highest = lax.Precision.HIGHEST
    out_real = (
        jnp.matmul(summed[0], cosine_table, precision=highest)
        + jnp.matmul(summed[1], sine_table, precision=highest)
    ) * factor
    out_imag = (
        jnp.matmul(summed[1], cosine_table, precision=highest)
        - jnp.matmul(summed[0], sine_table, precision=highest)
    ) * factor
    return jnp.stack([out_real, out_imag])


def on_device(signal, coarse_taps, fine_taps):
    length = signal.shape[1]
    history = (TAPS - 1) * CHANNELS
    cosine_table, sine_table = tables(CHANNELS)
    previous = from_behind(signal[:, length - history :], "tm", 1)
    extended = jnp.concatenate([previous, signal], axis=1)
    branches = coarse_branches(extended, coarse_taps, length)
    coarse = lax.all_to_all(
        coarse_spectrum(branches, cosine_table, sine_table),
        "tm",
        split_axis=1,
        concat_axis=2,
        tiled=True,
    )
    return fine_section(coarse, fine_taps)


def solution(mesh):
    return jax.shard_map(
        on_device,
        mesh=mesh,
        in_specs=(P(None, ("streams", "tm")), P(), P()),
        out_specs=P(None, "tm", "streams", None),
        check_vma=False,
    )
```

profile of v0, /device:TPU:0, one launch (start us, length us, event | category | flops | bytes accessed | tf_op | source)
XLA Modules:
  0.0 54.4 jit_solution(16357406457331470736)
XLA Ops:
  0.0 0.8 %slice.180 = f32[2,960]{1,0:T(2,128)S(1)} slice(f32[2,65536]{1,0:T(2,128)} %param.3), slice={[0:2], [64576:65536]} | slice | bytes 15360 | tf_op jit(solution)/shard_map/slice | solution.py:77
  0.8 2.4 %collective-permute-start = (f32[2,960]{1,0:T(2,128)S(1)}, f32[2,960]{1,0:T(2,128)S(1)}, u32[]{:S(2)}, u32[]{:S(2)}) collective-permute-start(f32[2,960]{1,0:T(2,128)S(1)} %slice.180), channel_id=1, source_target_pairs={{0,1},{1,2},{2,3},{4,5},{5,6},{6,7},{8,9},{9,10},{10,11},{12,13},{... | collective-permute-start | bytes 23048 | tf_op jit(solution)/shard_map/ppermute | solution.py:16
  3.2 1.0 %slice_bitcast_fusion.21 = (f32[64]{0:T(128)S(1)}, f32[64]{0:T(128)S(1)}, f32[64]{0:T(128)S(1)}, f32[64]{0:T(128)S(1)}, f32[64]{0:T(128)S(1)}, /*index=5*/f32[64...) fusion(f32[16,64]{1,0:T(8,128)} %param.4), kind=kLoop, calls=%fused_computation.166 | loop fusion | bytes 8192 | tf_op jit(solution)/shard_map/tile | solution.py:32
  5.6 4.7 %fusion.23 = (f32[1,2,512,128]{3,1,2,0:T(2,128)S(1)}, f32[1,2,512,128]{3,1,2,0:T(2,128)S(1)}, f32[1,2,512,128]{3,1,2,0:T(2,128)S(1)}, f32[1,2,512,128]{3,1,2,0:T...) fusion(f32[2,960]{1,0:T(2,128)S(1)} %collective-permute-done, f32[2,65536]{1,0:T(2,128)} %param.3), kind=kLoop, calls=%fused_computation.51 | loop fusion | flops 786432 | bytes 3677696
  10.3 2.6 %fusion.35 = (f32[1,2,512,128]{3,1,2,0:T(2,128)S(1)}, f32[1,2,512,128]{3,1,2,0:T(2,128)S(1)}, f32[1,2,512,128]{3,1,2,0:T(2,128)S(1)}, f32[1,2,512,128]{3,1,2,0:T...) fusion(f32[2,960]{1,0:T(2,128)S(1)} %collective-permute-done, f32[2,65536]{1,0:T(2,128)S(1)} %copy-done), kind=kLoop, calls=%fused_computation.63 | loop fusion | flops 786432 | bytes 3677696
  12.9 1.3 %fusion.47 = (f32[1,2,512,128]{3,1,2,0:T(2,128)S(1)}, f32[1,2,512,128]{3,1,2,0:T(2,128)S(1)}, f32[1,2,512,128]{3,1,2,0:T(2,128)S(1)}) fusion(f32[2,960]{1,0:T(2,128)S(1)} %collective-permute-done, f32[2,65536]{1,0:T(2,128)S(1)} %copy-done), kind=kLoop, calls=%fused_computation.75 | loop fusion | flops 393216 | bytes 2104832
  14.2 0.6 %fusion.66 = f32[2,512,128]{2,1,0:T(8,128)S(1)} fusion(f32[1,2,512,128]{3,1,2,0:T(2,128)S(1)} %get-tuple-element.18, f32[1,2,512,128]{3,1,2,0:T(2,128)S(1)} %get-tuple-element.19, f32[1,2,512,128]{3,1,2,0:T(2,128)S(1)} %get-tuple-element.17, f32[1,2,512,128]{3,1,2,0:T(2,128)S(1)} %get-tuple-element.16, f32[1,2,512,128]{3,1,2,0:T(2,128)S(1)} %get-tuple-element.15, ...), kind=kLoop, calls=%fused_computation.95 | loop fusion | flops 4063232 | bytes 8921088 | tf_op jit(solution)/shard_map/add | solution.py:32
  14.8 0.1 squeeze.16
  15.0 0.8 %fusion.98 = f32[64,1024]{1,0:T(8,128)S(1)} fusion(f32[1024,64]{1,0:T(8,128)S(1)} %squeeze.16), kind=kOutput, calls=%fused_computation.146 | convolution fusion | flops 50388992 | bytes 524288 | tf_op jit(solution)/shard_map/kp,tp->kt/dot_general | solution.py:40
  15.8 0.2 squeeze.17
  15.9 0.8 %fusion.96 = f32[64,1024]{1,0:T(8,128)S(1)} fusion(f32[1024,64]{1,0:T(8,128)S(1)} %squeeze.17), kind=kOutput, calls=%fused_computation.145 | convolution fusion | flops 50388992 | bytes 524288 | tf_op jit(solution)/shard_map/kp,tp->kt/dot_general | solution.py:44
  16.7 0.8 %fusion.3 = f32[1,64,1024]{2,1,0:T(8,128)S(1)} fusion(f32[64,1024]{1,0:T(8,128)S(1)} %fusion.98, f32[1024,64]{1,0:T(8,128)S(1)} %squeeze.17), kind=kOutput, calls=%fused_computation.29 | convolution fusion | flops 50520064 | bytes 786432 | tf_op jit(solution)/shard_map/kp,tp->kt/dot_general | solution.py:41
  17.5 0.8 %fusion.1 = f32[1,64,1024]{2,1,0:T(8,128)S(1)} fusion(f32[64,1024]{1,0:T(8,128)S(1)} %fusion.96, f32[1024,64]{1,0:T(8,128)S(1)} %squeeze.16), kind=kOutput, calls=%fused_computation.26 | convolution fusion | flops 50520064 | bytes 786432 | tf_op jit(solution)/shard_map/kp,tp->kt/dot_general | solution.py:45
  18.4 1.2 %copy.6 = f32[2,64,1024]{2,0,1:T(2,128)} copy(f32[2,64,1024]{2,1,0:T(8,128)S(1)} %pad_maximum_fusion.1) | data formatting | bytes 1048576 | tf_op jit(solution)/shard_map/stack | solution.py:47
  19.6 4.5 %all-to-all-start = ((f32[2,64,1024]{2,0,1:T(2,128)}), f32[2,64,1024]{2,0,1:T(2,128)S(1)}, u32[]{:S(2)}, u32[]{:S(2)}) async-start(f32[2,64,1024]{2,0,1:T(2,128)} %copy.6), calls=%async_computation | async-start | bytes 1048576 | tf_op jit(solution)/shard_map/all_to_all | solution.py:80
  24.1 8.8 %all-to-all-done = f32[2,64,1024]{2,0,1:T(2,128)S(1)} async-done(((f32[2,64,1024]{2,0,1:T(2,128)}), f32[2,64,1024]{2,0,1:T(2,128)S(1)}, u32[]{:S(2)}, u32[]{:S(2)}) %all-to-all-start) | async-done | bytes 524320 | tf_op jit(solution)/shard_map/all_to_all | solution.py:80
  32.9 0.3 copy.41
  33.3 0.2 reshape.109
  33.5 0.6 %fusion.59 = f32[2,16,8,512]{3,2,1,0:T(8,128)S(1)} fusion(f32[2,16,8,512]{3,2,1,0:T(8,128)S(1)} %reshape.109, f32[512]{0:T(512)S(1)} %bitcast.214, f32[512]{0:T(512)S(1)} %bitcast.215, f32[512]{0:T(512)S(1)} %bitcast.205, f32[512]{0:T(512)S(1)} %bitcast.206, f32[512]{0:T(512)S(1)} %bitcast.207, f32[512]{0:T(512)S(1)} %bitcast.208, f32[512]{0:T(512)S(1)} %bitcast.209, ...), kind=kLoop, calls=%fused_computation.87 | loop fusion | flops 2490368 | bytes 1073152 | tf_op jit(solution)/shard_map/add | solution.py:58
  34.1 4.9 %fusion.15 = f32[16,8,512]{2,1,0:T(8,128)S(1)} fusion(f32[2,16,8,512]{3,2,1,0:T(8,128)S(1)} %fusion.59), kind=kOutput, calls=%fused_computation.43 | convolution fusion | flops 406323200 | bytes 524288 | tf_op jit(solution)/shard_map/dot_general | solution.py:63
  39.0 4.9 %fusion.13 = f32[16,8,512]{2,1,0:T(8,128)S(1)} fusion(f32[2,16,8,512]{3,2,1,0:T(8,128)S(1)} %fusion.59), kind=kOutput, calls=%fused_computation.41 | convolution fusion | flops 406323200 | bytes 524288 | tf_op jit(solution)/shard_map/dot_general | solution.py:67
  43.8 4.9 %fusion.7 = f32[1,16,8,512]{3,2,1,0:T(8,128)S(1)} fusion(f32[16,8,512]{2,1,0:T(8,128)S(1)} %fusion.15, f32[2,16,8,512]{3,2,1,0:T(8,128)S(1)} %fusion.59), kind=kOutput, calls=%fused_computation.35 | convolution fusion | flops 406454272 | bytes 786432 | tf_op jit(solution)/shard_map/dot_general | solution.py:64
  48.7 4.9 %fusion.5 = f32[1,16,8,512]{3,2,1,0:T(8,128)S(1)} fusion(f32[16,8,512]{2,1,0:T(8,128)S(1)} %fusion.13, f32[2,16,8,512]{3,2,1,0:T(8,128)S(1)} %fusion.59), kind=kOutput, calls=%fused_computation.32 | convolution fusion | flops 406454272 | bytes 786432 | tf_op jit(solution)/shard_map/dot_general | solution.py:68
  53.6 0.8 %pad_maximum_fusion.2 = f32[2,16,8,512]{3,2,1,0:T(8,128)} fusion(f32[1,16,8,512]{3,2,1,0:T(8,128)S(1)} %fusion.5, f32[1,16,8,512]{3,2,1,0:T(8,128)S(1)} %fusion.7), kind=kLoop, calls=%fused_computation.128 | loop fusion | flops 131072 | bytes 1048576 | tf_op jit(solution)/shard_map/stack | solution.py:70
  (40 shorter events, 1.5 us)
Async XLA Ops:
  0.8 4.8 %collective-permute-start = (f32[2,960]{1,0:T(2,128)S(1)}, f32[2,960]{1,0:T(2,128)S(1)}, u32[]{:S(2)}, u32[]{:S(2)}) collective-permute-start(f32[2,960]{1,0:T(2,128)S(1)} %slice.180), channel_id=1, source_target_pairs={{0,1},{1,2},{2,3},{4,5},{5,6},{6,7},{8,9},{9,10},{10,11},{12,13},{... | collective-permute-start | bytes 23048 | tf_op jit(solution)/shard_map/ppermute | solution.py:16
  5.6 4.7 %copy-start = (f32[2,65536]{1,0:T(2,128)S(1)}, f32[2,65536]{1,0:T(2,128)}, u32[]{:S(2)}) copy-start(f32[2,65536]{1,0:T(2,128)} %param.3) | copy-start | bytes 1572868
  19.6 4.5 %copy-start.1 = (f32[12,512]{1,0:T(8,128)S(1)}, f32[12,512]{1,0:T(8,128)}, u32[]{:S(2)}) copy-start(f32[12,512]{1,0:T(8,128)} %param.5) | copy-start | bytes 73732
  19.6 13.3 %all-to-all-start = ((f32[2,64,1024]{2,0,1:T(2,128)}), f32[2,64,1024]{2,0,1:T(2,128)S(1)}, u32[]{:S(2)}, u32[]{:S(2)}) async-start(f32[2,64,1024]{2,0,1:T(2,128)} %copy.6), calls=%async_computation | async-start | bytes 1048576 | tf_op jit(solution)/shard_map/all_to_all | solution.py:80
where the time goes:
time: 54.7 us; the launch traced here: 54.4 us
  matrix products  22.7 us (41%)
  other arithmetic  10.6 us (19%)
  waiting for transfers between devices  8.79 us (16%)
  starting transfers between devices  6.89 us (13%)
  local copies, waits for them, and re-layouts  5.27 us (10%)
    all_to_all x1, waiting for transfers between devices, on_device(): lax.all_to_all(coarse_spectrum(branches, cosine_table, sine_table), 'tm',...  8.79 us
    unnamed x3, other arithmetic  8.52 us
    dot_general x1, matrix products, fine_section(): jnp.matmul(summed[0], cosine_table, precision=highest)  4.87 us
    dot_general x1, matrix products, fine_section(): jnp.matmul(summed[1], cosine_table, precision=highest)  4.87 us
    dot_general x1, matrix products, fine_section(): jnp.matmul(summed[0], sine_table, precision=highest)  4.86 us
    dot_general x1, matrix products, fine_section(): jnp.matmul(summed[1], sine_table, precision=highest)  4.86 us
    all_to_all x1, starting transfers between devices, on_device(): lax.all_to_all(coarse_spectrum(branches, cosine_table, sine_table), 'tm',...  4.5 us
    ppermute x1, starting transfers between devices, from_behind(): return lax.ppermute(array, axis, pairs)  2.39 us
  transfers between devices with their start and end apart: 2, of which 1 were waited for; matrix products, arithmetic and copies ran while one was open for 4% of the time, Pallas kernels for 0%

commit v1 on v0

--- a/solution.py
+++ b/solution.py
@@ -8,6 +8,17 @@
 FINE = 512
 TAPS = 16
 FINE_TAPS = 12
+
+
+def split_up(shard, dim, size):
+    before, after = (shard.shape[:dim], shard.shape[dim + 1 :])
+    return jnp.moveaxis(shard.reshape(*before, size, -1, *after), dim, 0)
+
+
+def joined_along(blocks, dim):
+    dims = list(blocks.shape[1:])
+    dims[dim] *= blocks.shape[0]
+    return jnp.moveaxis(blocks, 0, dim).reshape(dims)
 
 
 def from_behind(array, axis, by):
@@ -77,13 +88,15 @@
     previous = from_behind(signal[:, length - history :], "tm", 1)
     extended = jnp.concatenate([previous, signal], axis=1)
     branches = coarse_branches(extended, coarse_taps, length)
-    coarse = lax.all_to_all(
-        coarse_spectrum(branches, cosine_table, sine_table),
-        "tm",
-        split_axis=1,
-        concat_axis=2,
-        tiled=True,
-    )
+    x = coarse_spectrum(branches, cosine_table, sine_table)
+    peers, index = (lax.axis_size("tm"), lax.axis_index("tm"))
+    blocks = split_up(x, 1, peers)
+    outs = [blocks[index]]
+    for step in range(1, peers):
+        sent = blocks[index ^ step]
+        outs.append(lax.ppermute(sent, "tm", [(i_2, i_2 ^ step) for i_2 in range(peers)]))
+    blocks = jnp.stack(outs)[index ^ jnp.arange(peers)]
+    coarse = joined_along(blocks, 2)
     return fine_section(coarse, fine_taps)
 
 

time: 54.7 us -> 52.4 us (0.958)
  waiting for transfers between devices: 8.79 us -> 5.95 us
  other arithmetic: 10.6 us -> 11.7 us
  local copies, waits for them, and re-layouts: 5.27 us -> 4.65 us
    all_to_all x1 -> x0, waiting for transfers between devices: 8.79 us -> none  [on_device(): lax.all_to_all(coarse_spectrum(branches, cosine_table, sine_table), 'tm',...]
    ppermute x0 -> x3, waiting for transfers between devices: none -> 5.94 us  [on_device(): lax.ppermute(sent, 'tm', [(i_2, i_2 ^ step) for i_2 in range(peers)])]
    all_to_all x1 -> x0, starting transfers between devices: 4.5 us -> none  [on_device(): lax.all_to_all(coarse_spectrum(branches, cosine_table, sine_table), 'tm',...]
    ppermute x0 -> x3, starting transfers between devices: none -> 4.12 us  [on_device(): lax.ppermute(sent, 'tm', [(i_2, i_2 ^ step) for i_2 in range(peers)])]
    slice x1, other arithmetic: 0.02 us -> 1.04 us  [fine_section(): fine_taps[tap_index] * padded[:, :, offset:offset + fine_frames, :]]
    another operation x1, local copies, waits for them, and re-layouts: 1.2 us -> 0.21 us  [fine_section(): shaped = coarse.reshape(2, group_size, fine_frames, FINE)]
    gather x0 -> x1, local copies, waits for them, and re-layouts: none -> 0.58 us  [on_device(): blocks = jnp.stack(outs)[index ^ jnp.arange(peers)]]
  transfers between devices with their start and end apart: 2 -> 4, of which waited for: 1 -> 2; matrix products, arithmetic and copies ran while one was open for 4% -> 7% of each run, Pallas kernels for 0% -> 0%
where the time goes in v1:
time: 52.4 us; the launch traced here: 51.9 us
  matrix products  22.9 us (44%)
  other arithmetic  11.7 us (22%)
  starting transfers between devices  6.51 us (12%)
  waiting for transfers between devices  5.95 us (11%)
  local copies, waits for them, and re-layouts  4.65 us (9%)
    unnamed x3, other arithmetic  8.52 us
    ppermute x3, waiting for transfers between devices, on_device(): lax.ppermute(sent, 'tm', [(i_2, i_2 ^ step) for i_2 in range(peers)])  5.94 us
    dot_general x1, matrix products, fine_section(): jnp.matmul(summed[1], cosine_table, precision=highest)  5.05 us
    dot_general x1, matrix products, fine_section(): jnp.matmul(summed[0], cosine_table, precision=highest)  4.87 us
    dot_general x1, matrix products, fine_section(): jnp.matmul(summed[1], sine_table, precision=highest)  4.86 us
    dot_general x1, matrix products, fine_section(): jnp.matmul(summed[0], sine_table, precision=highest)  4.86 us
    ppermute x3, starting transfers between devices, on_device(): lax.ppermute(sent, 'tm', [(i_2, i_2 ^ step) for i_2 in range(peers)])  4.12 us
    ppermute x1, starting transfers between devices, from_behind(): return lax.ppermute(array, axis, pairs)  2.39 us
  transfers between devices with their start and end apart: 4, of which 2 were waited for; matrix products, arithmetic and copies ran while one was open for 7% of the time, Pallas kernels for 0%

profile of v1, /device:TPU:0, one launch (start us, length us, event | category | flops | bytes accessed | tf_op | source)
XLA Modules:
  0.0 51.9 jit_solution(1405505108227669346)
XLA Ops:
  0.0 0.8 %slice.180 = f32[2,960]{1,0:T(2,128)S(1)} slice(f32[2,65536]{1,0:T(2,128)} %param.3), slice={[0:2], [64576:65536]} | slice | bytes 15360 | tf_op jit(solution)/shard_map/slice | solution.py:88
  0.8 2.4 %collective-permute-start = (f32[2,960]{1,0:T(2,128)S(1)}, f32[2,960]{1,0:T(2,128)S(1)}, u32[]{:S(2)}, u32[]{:S(2)}) collective-permute-start(f32[2,960]{1,0:T(2,128)S(1)} %slice.180), channel_id=1, source_target_pairs={{0,1},{1,2},{2,3},{4,5},{5,6},{6,7},{8,9},{9,10},{10,11},{12,13},{... | collective-permute-start | bytes 23048 | tf_op jit(solution)/shard_map/ppermute | solution.py:27
  3.2 1.0 %fusion.142 = (f32[1,512]{1,0:T(1,128)S(1)}, f32[1,512]{1,0:T(1,128)S(1)}, f32[1,512]{1,0:T(1,128)S(1)}, f32[1,512]{1,0:T(1,128)S(1)}, f32[1,512]{1,0:T(1,128)S(...) fusion(f32[12,512]{1,0:T(8,128)} %param.5), kind=kLoop, calls=%fused_computation.217 | loop fusion | flops 2048 | bytes 49152 | tf_op jit(solution)/shard_map/slice | solution.py:69
  4.2 1.0 %slice_bitcast_fusion.21 = (f32[64]{0:T(128)S(1)}, f32[64]{0:T(128)S(1)}, f32[64]{0:T(128)S(1)}, f32[64]{0:T(128)S(1)}, f32[64]{0:T(128)S(1)}, /*index=5*/f32[64...) fusion(f32[16,64]{1,0:T(8,128)} %param.4), kind=kLoop, calls=%fused_computation.191 | loop fusion | bytes 8192 | tf_op jit(solution)/shard_map/tile | solution.py:43
  6.7 4.7 %fusion.21 = (f32[1,2,512,128]{3,1,2,0:T(2,128)S(1)}, f32[1,2,512,128]{3,1,2,0:T(2,128)S(1)}, f32[1,2,512,128]{3,1,2,0:T(2,128)S(1)}, f32[1,2,512,128]{3,1,2,0:T...) fusion(f32[2,960]{1,0:T(2,128)S(1)} %collective-permute-done, f32[2,65536]{1,0:T(2,128)} %param.3), kind=kLoop, calls=%fused_computation.58 | loop fusion | flops 786432 | bytes 3677696
  11.3 2.6 %fusion.33 = (f32[1,2,512,128]{3,1,2,0:T(2,128)S(1)}, f32[1,2,512,128]{3,1,2,0:T(2,128)S(1)}, f32[1,2,512,128]{3,1,2,0:T(2,128)S(1)}, f32[1,2,512,128]{3,1,2,0:T...) fusion(f32[2,960]{1,0:T(2,128)S(1)} %collective-permute-done, f32[2,65536]{1,0:T(2,128)S(1)} %copy-done), kind=kLoop, calls=%fused_computation.70 | loop fusion | flops 786432 | bytes 3677696
  13.9 1.3 %fusion.45 = (f32[1,2,512,128]{3,1,2,0:T(2,128)S(1)}, f32[1,2,512,128]{3,1,2,0:T(2,128)S(1)}, f32[1,2,512,128]{3,1,2,0:T(2,128)S(1)}) fusion(f32[2,960]{1,0:T(2,128)S(1)} %collective-permute-done, f32[2,65536]{1,0:T(2,128)S(1)} %copy-done), kind=kLoop, calls=%fused_computation.82 | loop fusion | flops 393216 | bytes 2104832
  15.2 0.6 %fusion.64 = f32[2,512,128]{2,1,0:T(8,128)S(1)} fusion(f32[1,2,512,128]{3,1,2,0:T(2,128)S(1)} %get-tuple-element.18, f32[1,2,512,128]{3,1,2,0:T(2,128)S(1)} %get-tuple-element.19, f32[1,2,512,128]{3,1,2,0:T(2,128)S(1)} %get-tuple-element.17, f32[1,2,512,128]{3,1,2,0:T(2,128)S(1)} %get-tuple-element.16, f32[1,2,512,128]{3,1,2,0:T(2,128)S(1)} %get-tuple-element.15, ...), kind=kLoop, calls=%fused_computation.102 | loop fusion | flops 4063232 | bytes 8921088 | tf_op jit(solution)/shard_map/add | solution.py:43
  16.0 0.8 %fusion.102 = f32[64,1024]{1,0:T(8,128)S(1)} fusion(f32[1024,64]{1,0:T(8,128)S(1)} %squeeze.26), kind=kOutput, calls=%fused_computation.159 | convolution fusion | flops 50388992 | bytes 524288 | tf_op jit(solution)/shard_map/kp,tp->kt/dot_general | solution.py:55
  17.0 0.8 %fusion.104 = f32[64,1024]{1,0:T(8,128)S(1)} fusion(f32[1024,64]{1,0:T(8,128)S(1)} %squeeze.25), kind=kOutput, calls=%fused_computation.160 | convolution fusion | flops 50388992 | bytes 524288 | tf_op jit(solution)/shard_map/kp,tp->kt/dot_general | solution.py:51
  17.8 0.8 %fusion = f32[64,1024]{1,0:T(8,128)S(1)} fusion(f32[64,1024]{1,0:T(8,128)S(1)} %fusion.102, f32[1024,64]{1,0:T(8,128)S(1)} %squeeze.25), kind=kOutput, calls=%fused_computation.26 | convolution fusion | flops 50520064 | bytes 786432 | tf_op jit(solution)/shard_map/kp,tp->kt/dot_general | solution.py:56
  18.6 0.8 %fusion.1 = f32[64,1024]{1,0:T(8,128)S(1)} fusion(f32[64,1024]{1,0:T(8,128)S(1)} %fusion.104, f32[1024,64]{1,0:T(8,128)S(1)} %squeeze.26), kind=kOutput, calls=%fused_computation.28 | convolution fusion | flops 50520064 | bytes 786432 | tf_op jit(solution)/shard_map/kp,tp->kt/dot_general | solution.py:52
  19.5 2.7 %collective-permute-start.1 = (f32[2,16,1024]{2,1,0:T(8,128)S(1)}, f32[2,16,1024]{2,1,0:T(8,128)S(1)}, u32[]{:S(2)}, u32[]{:S(2)}) collective-permute-start(f32[2,16,1024]{2,1,0:T(8,128)S(1)} %get-tuple-element.21), channel_id=1, source_target_pairs={{0,1},{1,0},{2,3},{3,2},{4,5},{5,4},{6,7},{7,6},{8,9},{9,8},{10,11... | collective-permute-start | bytes 393224 | tf_op jit(solution)/shard_map/ppermute | solution.py:97
  22.2 1.4 %collective-permute-start.3 = (f32[2,16,1024]{2,1,0:T(8,128)S(1)}, f32[2,16,1024]{2,1,0:T(8,128)S(1)}, u32[]{:S(2)}, u32[]{:S(2)}) collective-permute-start(f32[2,16,1024]{2,1,0:T(8,128)S(1)} %get-tuple-element.23), channel_id=1, source_target_pairs={{0,3},{1,2},{2,1},{3,0},{4,7},{5,6},{6,5},{7,4},{8,11},{9,10},{10,... | collective-permute-start | bytes 393224 | tf_op jit(solution)/shard_map/ppermute | solution.py:97
  23.6 4.9 %collective-permute-done.2 = f32[2,16,1024]{2,1,0:T(8,128)S(1)} collective-permute-done((f32[2,16,1024]{2,1,0:T(8,128)S(1)}, f32[2,16,1024]{2,1,0:T(8,128)S(1)}, u32[]{:S(2)}, u32[]{:S(2)}) %collective-permute-start.2) | collective-permute-done | bytes 131104 | tf_op jit(solution)/shard_map/ppermute | solution.py:97
  28.5 1.0 %collective-permute-done.3 = f32[2,16,1024]{2,1,0:T(8,128)S(1)} collective-permute-done((f32[2,16,1024]{2,1,0:T(8,128)S(1)}, f32[2,16,1024]{2,1,0:T(8,128)S(1)}, u32[]{:S(2)}, u32[]{:S(2)}) %collective-permute-start.3) | collective-permute-done | bytes 131104 | tf_op jit(solution)/shard_map/ppermute | solution.py:97
  29.6 0.6 %gather_fusion = f32[4,2,16,1024]{3,2,1,0:T(8,128)S(1)} fusion(f32[4,2,16,1024]{3,2,1,0:T(8,128)S(1)} %pad_maximum_fusion.1, s32[1024]{0:T(1024)S(1)} %pad_clamp_fusion), kind=kCustom, calls=%fused_computation | custom fusion | bytes 1048592 | tf_op jit(solution)/shard_map/gather | solution.py:98
  30.2 0.3 copy.4
  30.8 0.6 %fusion.57 = f32[2,16,8,512]{3,2,1,0:T(8,128)S(1)} fusion(f32[2,16,8,512]{3,2,1,0:T(8,128)S(1)} %reshape_reshape.3, f32[512]{0:T(512)S(1)} %bitcast.226, f32[512]{0:T(512)S(1)} %bitcast.227, f32[512]{0:T(512)S(1)} %bitcast.217, f32[512]{0:T(512)S(1)} %bitcast.218, f32[512]{0:T(512)S(1)} %bitcast.219, f32[512]{0:T(512)S(1)} %bitcast.220, ...), kind=kLoop, calls=%fused_computation.94 | loop fusion | flops 2490368 | bytes 1073152 | tf_op jit(solution)/shard_map/add | solution.py:69
  31.3 4.9 %fusion.13 = f32[16,8,512]{2,1,0:T(8,128)S(1)} fusion(f32[2,16,8,512]{3,2,1,0:T(8,128)S(1)} %fusion.57), kind=kOutput, calls=%fused_computation.42 | convolution fusion | flops 406323200 | bytes 524288 | tf_op jit(solution)/shard_map/dot_general | solution.py:74
  36.2 5.1 %fusion.11 = f32[16,8,512]{2,1,0:T(8,128)S(1)} fusion(f32[2,16,8,512]{3,2,1,0:T(8,128)S(1)} %fusion.57), kind=kOutput, calls=%fused_computation.40 | convolution fusion | flops 406323200 | bytes 524288 | tf_op jit(solution)/shard_map/dot_general | solution.py:78
  41.3 4.9 %fusion.5 = f32[1,16,8,512]{3,2,1,0:T(8,128)S(1)} fusion(f32[16,8,512]{2,1,0:T(8,128)S(1)} %fusion.13, f32[2,16,8,512]{3,2,1,0:T(8,128)S(1)} %fusion.57), kind=kOutput, calls=%fused_computation.34 | convolution fusion | flops 406454272 | bytes 786432 | tf_op jit(solution)/shard_map/dot_general | solution.py:75
  46.2 4.9 %fusion.3 = f32[1,16,8,512]{3,2,1,0:T(8,128)S(1)} fusion(f32[16,8,512]{2,1,0:T(8,128)S(1)} %fusion.11, f32[2,16,8,512]{3,2,1,0:T(8,128)S(1)} %fusion.57), kind=kOutput, calls=%fused_computation.31 | convolution fusion | flops 406454272 | bytes 786432 | tf_op jit(solution)/shard_map/dot_general | solution.py:79
  51.0 0.8 %pad_maximum_fusion.2 = f32[2,16,8,512]{3,2,1,0:T(8,128)} fusion(f32[1,16,8,512]{3,2,1,0:T(8,128)S(1)} %fusion.3, f32[1,16,8,512]{3,2,1,0:T(8,128)S(1)} %fusion.5), kind=kLoop, calls=%fused_computation.135 | loop fusion | flops 131072 | bytes 1048576 | tf_op jit(solution)/shard_map/stack | solution.py:81
  (45 shorter events, 2.0 us)
Async XLA Ops:
  0.8 5.9 %collective-permute-start = (f32[2,960]{1,0:T(2,128)S(1)}, f32[2,960]{1,0:T(2,128)S(1)}, u32[]{:S(2)}, u32[]{:S(2)}) collective-permute-start(f32[2,960]{1,0:T(2,128)S(1)} %slice.180), channel_id=1, source_target_pairs={{0,1},{1,2},{2,3},{4,5},{5,6},{6,7},{8,9},{9,10},{10,11},{12,13},{... | collective-permute-start | bytes 23048 | tf_op jit(solution)/shard_map/ppermute | solution.py:27
  6.7 4.7 %copy-start = (f32[2,65536]{1,0:T(2,128)S(1)}, f32[2,65536]{1,0:T(2,128)}, u32[]{:S(2)}) copy-start(f32[2,65536]{1,0:T(2,128)} %param.3) | copy-start | bytes 1572868
  19.5 4.1 %collective-permute-start.1 = (f32[2,16,1024]{2,1,0:T(8,128)S(1)}, f32[2,16,1024]{2,1,0:T(8,128)S(1)}, u32[]{:S(2)}, u32[]{:S(2)}) collective-permute-start(f32[2,16,1024]{2,1,0:T(8,128)S(1)} %get-tuple-element.21), channel_id=1, source_target_pairs={{0,1},{1,0},{2,3},{3,2},{4,5},{5,4},{6,7},{7,6},{8,9},{9,8},{10,11... | collective-permute-start | bytes 393224 | tf_op jit(solution)/shard_map/ppermute | solution.py:97
  22.2 6.4 %collective-permute-start.2 = (f32[2,16,1024]{2,1,0:T(8,128)S(1)}, f32[2,16,1024]{2,1,0:T(8,128)S(1)}, u32[]{:S(2)}, u32[]{:S(2)}) collective-permute-start(f32[2,16,1024]{2,1,0:T(8,128)S(1)} %get-tuple-element.22), channel_id=1, source_target_pairs={{0,2},{1,3},{2,0},{3,1},{4,6},{5,7},{6,4},{7,5},{8,10},{9,11},{10,... | collective-permute-start | bytes 393224 | tf_op jit(solution)/shard_map/ppermute | solution.py:97
  22.2 7.4 %collective-permute-start.3 = (f32[2,16,1024]{2,1,0:T(8,128)S(1)}, f32[2,16,1024]{2,1,0:T(8,128)S(1)}, u32[]{:S(2)}, u32[]{:S(2)}) collective-permute-start(f32[2,16,1024]{2,1,0:T(8,128)S(1)} %get-tuple-element.23), channel_id=1, source_target_pairs={{0,3},{1,2},{2,1},{3,0},{4,7},{5,6},{6,5},{7,4},{8,11},{9,10},{10,... | collective-permute-start | bytes 393224 | tf_op jit(solution)/shard_map/ppermute | solution.py:97
